TPU v7x, 128 devices: a whole 4x4x4 slice. The times are simulated.
128 devices in a mesh: req: 32 (over x, y, core), mlp: 4 (over z).
Axes of the slice: x: 4, y: 4, z: 4, core: 2. Of those that a mesh axis runs over, the one named last changes fastest.
Arguments:
- tokens: bfloat16 [1024, 2048], P('req'), may hold values from -6 to 6
- prefix_len: int32 [32], replicated, may hold values from 1 to 4096, 65536 in all
- tail_len: int32 [32, 16], replicated, may hold values from 1 to 64, 512 in all within a row
- tail_src: int32 [512], replicated, may hold values from 0 to 31, as said below
- prefix_kv: bfloat16 [32, 2, 4096, 2048], P('req', None, None, 'mlp'), may hold values from -256 to 256, as said below
- tail_kv: bfloat16 [512, 2, 64, 2048], P('req', None, None, 'mlp'), may hold values from -256 to 256, as said below
- w_qkv: bfloat16 [2048, 3, 2048], P(None, None, 'mlp'), may hold values from -0.125 to 0.125
- w_out: bfloat16 [2048, 2048], P('mlp'), may hold values from -0.125 to 0.125
- w_gate: bfloat16 [8192, 2048], P(('req', 'mlp')), may hold values from -0.125 to 0.125
- w_up: bfloat16 [8192, 2048], P(('req', 'mlp')), may hold values from -0.125 to 0.125
- w_down: bfloat16 [8192, 2048], P(('req', 'mlp')), may hold values from -0.0625 to 0.0625
- w_score: float32 [2048], replicated, may hold values from -0.125 to 0.125
Outputs:
- layer_out: bfloat16 [1024, 2048], P(('req', 'mlp'))
- score: float32 [1024], P(('req', 'mlp'))
Inputs may be any that keep to these rules, and one draw needn't show every extreme that they name: tail_src[c] is the req index whose shard of tail_kv holds the tail of continuation c; each device holds 16 tails, in increasing order of continuation. The 16 continuations of a prompt come in groups of 1 from 16 different devices, so from one device to the device of one prompt goes exactly one tail or none. `prefix_kv`: keys are already rotated. `tail_kv`: keys are already rotated.
All inputs are finite; a program needn't handle non-finite values.
Results may differ from a plain program's by a relative error of at most 0.027.
Values may be sent and summed in bfloat16 or wider, within the bound.
A program may use at most 128 MiB of HBM per device.

v0:
```python
from functools import reduce
import jax
import jax.numpy as jnp
from jax import lax
from jax.sharding import PartitionSpec as P

HEAD_DIM = 128
CONT = 16
NEW = 2


def layer_norm(values):
    centre = values - jnp.mean(values, axis=-1, keepdims=True)
    spread = jnp.mean(centre * centre, axis=-1, keepdims=True)
    return centre * lax.rsqrt(spread + 1e-05)


def rotate(vectors, positions):
    half_dim = vectors.shape[-1] // 2
    exponent = jnp.arange(half_dim, dtype=jnp.float32) * (2.0 / vectors.shape[-1])
    frequency = jnp.power(10000.0, -exponent)
    phase_radians = positions.astype(jnp.float32)[:, None] * frequency[None, :]
    cosine = jnp.cos(phase_radians)[:, None, :]
    sine_part = jnp.sin(phase_radians)[:, None, :]
    leading = vectors[..., :half_dim]
    trailing = vectors[..., half_dim:]
    return jnp.concatenate(
        [leading * cosine - trailing * sine_part, trailing * cosine + leading * sine_part], axis=-1
    )


def attend(queries, key_rows, values, key_mask):
    scaling = queries.shape[-1] ** (-0.5)
    scores = (
        jnp.einsum("cjhe,ckhe->cjhk", queries, key_rows, preferred_element_type=jnp.float32)
        * scaling
    )
    scores = jnp.where(key_mask, scores, -1e30)
    row_max = jnp.max(scores, axis=-1)
    weights = jnp.where(key_mask, jnp.exp(scores - row_max[..., None]), 0.0)
    row_sum = jnp.sum(weights, axis=-1)
    output = jnp.einsum(
        "cjhk,ckhe->cjhe", weights.astype(jnp.bfloat16), values, preferred_element_type=jnp.float32
    )
    return (row_max, row_sum, output)


def tail_attend(queries, cache_rows, lengths):
    local_heads = queries.shape[2]
    shaped = (cache_rows.shape[0], cache_rows.shape[2], local_heads, HEAD_DIM)
    key_rows = cache_rows[:, 0].reshape(shaped)
    value_rows = cache_rows[:, 1].reshape(shaped)
    tail_mask = (jnp.arange(cache_rows.shape[2], dtype=jnp.int32)[None, :] < lengths[:, None])[
        :, None, None, :
    ]
    return attend(queries, key_rows, value_rows, tail_mask)


def combine(pieces):
    overall = reduce(jnp.maximum, [piece[0] for piece in pieces])
    numerator = jnp.zeros_like(pieces[0][2])
    denominator = jnp.zeros_like(pieces[0][1])
    for piece in pieces:
        scale_factor = jnp.exp(piece[0] - overall)
        numerator = numerator + scale_factor[..., None] * piece[2]
        denominator = denominator + scale_factor * piece[1]
    return numerator / denominator[..., None]


def swiglu(normed, gate_rows, up_rows, down_rows):
    contract = (((1,), (1,)), ((), ()))
    gate_out = lax.dot_general(normed, gate_rows, contract, preferred_element_type=jnp.float32)
    up_out = lax.dot_general(normed, up_rows, contract, preferred_element_type=jnp.float32)
    hidden = (jax.nn.silu(gate_out) * up_out).astype(jnp.bfloat16)
    return jnp.dot(hidden, down_rows, preferred_element_type=jnp.float32)


def on_device(
    tokens,
    prefix_len,
    tail_len,
    tail_src,
    prefix_kv,
    tail_kv,
    w_qkv,
    w_out,
    w_gate,
    w_up,
    w_down,
    w_score,
):
    req_index = lax.axis_index("req")
    req_count = lax.axis_size("req")
    cap_rows = max(1, CONT // req_count)
    tok_count = tokens.shape[0]
    head_width = w_qkv.shape[2]
    local_heads = head_width // HEAD_DIM
    prefix_size = prefix_kv.shape[2]
    grouped = (CONT, NEW, local_heads, HEAD_DIM)
    normed = layer_norm(tokens.astype(jnp.float32)).astype(jnp.bfloat16)
    projected = jnp.einsum("td,dcf->tcf", normed, w_qkv, preferred_element_type=jnp.float32)
    own_prefix = lax.dynamic_index_in_dim(prefix_len, req_index, 0, keepdims=False)
    own_tails = lax.dynamic_index_in_dim(tail_len, req_index, 0, keepdims=False)
    offsets = jnp.arange(NEW, dtype=jnp.int32)
    positions = (own_prefix + own_tails[:, None] + offsets[None, :]).reshape(-1)
    queries = rotate(projected[:, 0].reshape(tok_count, local_heads, HEAD_DIM), positions).astype(
        jnp.bfloat16
    )
    new_keys = rotate(projected[:, 1].reshape(tok_count, local_heads, HEAD_DIM), positions).astype(
        jnp.bfloat16
    )
    new_values = projected[:, 2].astype(jnp.bfloat16)
    prefix_keys = prefix_kv[0, 0].reshape(1, prefix_size, local_heads, HEAD_DIM)
    prefix_values = prefix_kv[0, 1].reshape(1, prefix_size, local_heads, HEAD_DIM)
    prefix_mask = (jnp.arange(prefix_size, dtype=jnp.int32) < own_prefix)[None, None, None, :]
    prefix_part = attend(
        queries.reshape(1, tok_count, local_heads, HEAD_DIM),
        prefix_keys,
        prefix_values,
        prefix_mask,
    )
    prefix_part = tuple((member.reshape((CONT, NEW) + member.shape[2:]) for member in prefix_part))
    conts_all = tail_src.shape[0]
    indices = jnp.arange(conts_all, dtype=jnp.int32)
    owners = indices // CONT
    paired = (
        (tail_src[None, :] == tail_src[:, None])
        & (owners[None, :] == owners[:, None])
        & (indices[None, :] < indices[:, None])
    )
    pair_rank = jnp.sum(paired.astype(jnp.int32), axis=1)
    held_ids = jnp.nonzero(tail_src == req_index, size=CONT)[0].astype(jnp.int32)
    send_slots = owners[held_ids] * cap_rows + pair_rank[held_ids]
    own_ids = req_index * CONT + jnp.arange(CONT, dtype=jnp.int32)
    recv_slots = tail_src[own_ids] * cap_rows + pair_rank[own_ids]
    slots_total = req_count * cap_rows
    outgoing = (
        jnp.zeros((slots_total,) + tail_kv.shape[1:], jnp.bfloat16).at[send_slots].set(tail_kv)
    )
    incoming = lax.all_to_all(outgoing, "req", split_axis=0, concat_axis=0, tiled=True)
    fetched = incoming[recv_slots]
    tail_part = tail_attend(queries.reshape(grouped), fetched, own_tails)
    new_mask = (offsets[:, None] >= offsets[None, :])[None, :, None, :]
    new_part = attend(
        queries.reshape(grouped), new_keys.reshape(grouped), new_values.reshape(grouped), new_mask
    )
    attn_mix = (
        combine([prefix_part, tail_part, new_part])
        .reshape(tok_count, head_width)
        .astype(jnp.bfloat16)
    )
    partial_value = jnp.dot(attn_mix, w_out, preferred_element_type=jnp.float32)
    summed = lax.psum(partial_value, "mlp")
    residual = (tokens.astype(jnp.float32) + summed).astype(jnp.bfloat16)
    normed_mid = layer_norm(residual.astype(jnp.float32)).astype(jnp.bfloat16)
    row_share = tok_count // lax.axis_size("mlp")
    mlp_index = lax.axis_index("mlp")
    collected_entries = lax.all_gather(normed_mid, "req", axis=0, tiled=True)
    mlp_sum = lax.psum_scatter(
        swiglu(collected_entries, w_gate, w_up, w_down),
        ("req", "mlp"),
        scatter_dimension=0,
        tiled=True,
    )
    own_rows = lax.dynamic_slice_in_dim(residual, mlp_index * row_share, row_share, 0)
    layer_f32 = own_rows.astype(jnp.float32) + mlp_sum
    layer_out = layer_f32.astype(jnp.bfloat16)
    score = jnp.sum(layer_norm(layer_f32) * w_score[None, :], axis=-1)
    return (layer_out, score)


def solution(mesh):
    in_specs = (
        P("req", None),
        P(),
        P(),
        P(),
        P("req", None, None, "mlp"),
        P("req", None, None, "mlp"),
        P(None, None, "mlp"),
        P("mlp", None),
        P(("req", "mlp"), None),
        P(("req", "mlp"), None),
        P(("req", "mlp"), None),
        P(),
    )
    out_specs = (P(("req", "mlp"), None), P(("req", "mlp")))
    return jax.shard_map(
        on_device, mesh=mesh, in_specs=in_specs, out_specs=out_specs, check_vma=False
    )
```

profile of v0, /device:TPU:0, one launch (start us, length us, event | category | flops | bytes accessed | tf_op | source)
XLA Modules:
  0.0 868.8 jit_solution(6250330086719967981)
XLA Ops:
  7.2 1.5 convert_reduce_fusion.3
  10.4 4.1 scatter_custom_fusion
  16.9 2.4 broadcast_in_dim.121
  19.3 6.0 scatter_fusion
  25.3 7.7 all-to-all-start
  36.5 4.0 fusion.34
  42.5 5.7 fusion.78
  48.2 6.4 copy.222
  55.3 4.4 fusion.84
  59.7 2.1 fusion.3
  62.1 6.4 copy.225
  69.0 4.4 fusion.10
  73.4 12.4 %all-to-all-done = bf16[32,2,64,512]{3,2,1,0:T(8,128)(2,1)} async-done(((bf16[32,2,64,512]{3,2,1,0:T(8,128)(2,1)}), bf16[32,2,64,512]{3,2,1,0:T(8,128)(2,1)}, u32[]{:S(2)}, u32[]{:S(2)}) %all-to-all-start) | async-done | bytes 4194336 | tf_op jit(solution)/shard_map/all_to_all | solution.py:140
  85.7 4.2 gather_fusion.4
  90.0 2.7 fusion.79
  92.7 2.2 reshape_squeeze.15
  94.9 2.0 fusion.83
  99.7 1.7 fusion.12
  103.6 43.6 %all-reduce.2.cloned.1.call-done = f32[32,2048]{1,0:T(8,128)} async-done(((f32[32,2048]{1,0:T(8,128)}), f32[32,2048]{1,0:T(8,128)}) %all-reduce.2.cloned.1.call-update) | async-done | bytes 262160 | tf_op jit(solution)/shard_map/psum | solution.py:153
  149.4 46.5 %all-gather.2.cloned.1.call-done = bf16[1024,2048]{1,0:T(8,128)(2,1)} async-done(((bf16[32,2048]{1,0:T(8,128)(2,1)}), bf16[1024,2048]{1,0:T(8,128)(2,1)}) %all-gather.2.cloned.1.call-update) | async-done | bytes 4194320 | tf_op jit(solution)/shard_map/all_gather | solution.py:158
  195.9 3.6 fusion.85
  199.5 8.0 fusion.6
  207.5 650.6 %reduce-scatter.2.cloned.1.call-done = f32[8,2048]{1,0:T(8,128)} async-done(((f32[1024,2048]{1,0:T(8,128)}), f32[8,2048]{1,0:T(8,128)}) %reduce-scatter.2.cloned.1.call-update) | async-done | bytes 65552 | tf_op jit(solution)/shard_map/reduce_scatter | solution.py:159
  860.2 2.1 multiply_reduce_fusion
  (102 shorter events, 20.3 us)
Async XLA Ops:
  7.2 95.1 %copy-start = (bf16[512,2048]{1,0:T(8,128)(2,1)S(1)}, bf16[512,2048]{1,0:T(8,128)(2,1)}, u32[]{:S(2)}) copy-start(bf16[512,2048]{1,0:T(8,128)(2,1)} %param.19) | copy-start | bytes 6291460
  25.3 8.5 copy-start.1
  25.3 9.2 %copy-start.9 = (s32[32]{0:T(128)S(1)}, s32[32]{0:T(128)}, u32[]{:S(2)}) copy-start(s32[32]{0:T(128)} %param.13) | copy-start | bytes 388
  25.3 9.8 %copy-start.8 = (s32[32,16]{0,1:T(8,128)S(1)}, s32[32,16]{0,1:T(8,128)}, u32[]{:S(2)}) copy-start(s32[32,16]{0,1:T(8,128)} %param.14) | copy-start | bytes 6148
  25.3 10.0 %copy-start.2 = (bf16[32,2048]{1,0:T(8,128)(2,1)S(1)}, bf16[32,2048]{1,0:T(8,128)(2,1)}, u32[]{:S(2)}) copy-start(bf16[32,2048]{1,0:T(8,128)(2,1)} %param.12) | copy-start | bytes 393220
  25.3 60.4 %all-to-all-start = ((bf16[32,2,64,512]{3,2,1,0:T(8,128)(2,1)}), bf16[32,2,64,512]{3,2,1,0:T(8,128)(2,1)}, u32[]{:S(2)}, u32[]{:S(2)}) async-start(bf16[32,2,64,512]{3,2,1,0:T(8,128)(2,1)} %scatter_fusion), calls=%async_computation | async-start | bytes 8388608 | tf_op jit(solution)/shard_map/all_to_all | solution.py:140
  33.0 114.2 %all-reduce.2.cloned.1.call-start = ((), (), s32[]{:S(2)}) async-start(), calls=%async_computation.2 | async-start | bytes 524288 | tf_op jit(solution)/shard_map/psum | solution.py:153
  68.8 26.1 %copy-start.6 = (pred[16,64]{1,0:T(8,128)(4,1)}, pred[16,64]{1,0:T(8,128)(4,1)S(1)}, u32[]{:S(2)}) copy-start(pred[16,64]{1,0:T(8,128)(4,1)S(1)} %iota_compare_fusion.3) | copy-start | bytes 3076
  99.7 96.2 %copy-start.3 = (bf16[64,2048]{1,0:T(8,128)(2,1)S(1)}, bf16[64,2048]{1,0:T(8,128)(2,1)}, u32[]{:S(2)}) copy-start(bf16[64,2048]{1,0:T(8,128)(2,1)} %param.20) | copy-start | bytes 786436
  102.3 97.2 %copy-start.4 = (bf16[64,2048]{1,0:T(8,128)(2,1)S(1)}, bf16[64,2048]{1,0:T(8,128)(2,1)}, u32[]{:S(2)}) copy-start(bf16[64,2048]{1,0:T(8,128)(2,1)} %param.22) | copy-start | bytes 786436
  102.3 97.2 %copy-start.5 = (bf16[64,2048]{1,0:T(8,128)(2,1)S(1)}, bf16[64,2048]{1,0:T(8,128)(2,1)}, u32[]{:S(2)}) copy-start(bf16[64,2048]{1,0:T(8,128)(2,1)} %param.21) | copy-start | bytes 786436
  103.5 92.4 %all-gather.2.cloned.1.call-start = ((), (), s32[]{:S(2)}) async-start(), calls=%async_computation.3 | async-start | bytes 4325376 | tf_op jit(solution)/shard_map/all_gather | solution.py:158
  149.2 708.9 %reduce-scatter.2.cloned.1.call-start = ((), (), s32[]{:S(2)}) async-start(), calls=%async_computation.4 | async-start | bytes 8454144 | tf_op jit(solution)/shard_map/reduce_scatter | solution.py:159
  207.5 652.7 %copy-start.7 = (f32[2048]{0:T(1024)S(1)}, f32[2048]{0:T(1024)}, u32[]{:S(2)}) copy-start(f32[2048]{0:T(1024)} %param.23) | copy-start | bytes 24580
Sparse Core Ops, SparseCore 0:
  103.6 43.4 all-reduce.1
  149.6 46.2 all-gather.1
  207.6 650.4 reduce-scatter.1
where the time goes:
time: 870 us; the launch traced here: 869 us
  waiting for transfers between devices  753 us (87%)
  local copies, waits for them, and re-layouts  42.9 us (5%)
  matrix products  29.6 us (3%)
  other arithmetic  21.2 us (2%)
  between operations  14 us (2%)
    reduce_scatter x1, waiting for transfers between devices, on_device(): lax.psum_scatter(swiglu(collected_entries, w_gate, w_up, w_down), ('req',...  651 us
    all_gather x1, waiting for transfers between devices, on_device(): collected_entries = lax.all_gather(normed_mid, 'req', axis=0, tiled=True)  46.5 us
    psum x1, waiting for transfers between devices, on_device(): summed = lax.psum(partial_value, 'mlp')  43.6 us
  transfers between devices with their start and end apart: 4, of which 4 were waited for; matrix products, arithmetic and copies ran while one was open for 5% of the time, Pallas kernels for 0%

commit v1 on v0

--- a/solution.py
+++ b/solution.py
@@ -150,7 +150,9 @@
         .astype(jnp.bfloat16)
     )
     partial_value = jnp.dot(attn_mix, w_out, preferred_element_type=jnp.float32)
-    summed = lax.psum(partial_value, "mlp")
+    summed = partial_value
+    for hop in (1, 2):
+        summed = summed + lax.ppermute(summed, "mlp", [(dev, dev ^ hop) for dev in range(4)])
     residual = (tokens.astype(jnp.float32) + summed).astype(jnp.bfloat16)
     normed_mid = layer_norm(residual.astype(jnp.float32)).astype(jnp.bfloat16)
     row_share = tok_count // lax.axis_size("mlp")

time: 870 us -> 843 us (0.969)
  waiting for transfers between devices: 753 us -> 722 us
    psum x1 -> x0, waiting for transfers between devices: 43.6 us -> none  [on_device(): summed = lax.psum(partial_value, 'mlp')]
    ppermute x0 -> x2, waiting for transfers between devices: none -> 11.3 us  [on_device(): lax.ppermute(summed, 'mlp', [(dev, dev ^ hop) for dev in range(4)])]
  transfers between devices with their start and end apart: 4 -> 5, of which waited for: 4 -> 5; matrix products, arithmetic and copies ran while one was open for 5% -> 5% of each run, Pallas kernels for 0% -> 0%
where the time goes in v1:
time: 843 us; the launch traced here: 842 us
  waiting for transfers between devices  722 us (86%)
  local copies, waits for them, and re-layouts  42.9 us (5%)
  matrix products  28.9 us (3%)
  other arithmetic  20.4 us (2%)
  between operations  14.3 us (2%)
  starting transfers between devices  13.7 us (2%)
    reduce_scatter x1, waiting for transfers between devices, on_device(): lax.psum_scatter(swiglu(collected_entries, w_gate, w_up, w_down), ('req',...  652 us
    all_gather x1, waiting for transfers between devices, on_device(): collected_entries = lax.all_gather(normed_mid, 'req', axis=0, tiled=True)  46.8 us
  transfers between devices with their start and end apart: 5, of which 5 were waited for; matrix products, arithmetic and copies ran while one was open for 5% of the time, Pallas kernels for 0%

profile of v1, /device:TPU:0, one launch (start us, length us, event | category | flops | bytes accessed | tf_op | source)
XLA Modules:
  0.0 842.2 jit_solution(12766358479816505497)
XLA Ops:
  10.4 4.1 scatter_custom_fusion
  16.9 2.4 broadcast_in_dim.121
  19.3 6.0 scatter_fusion
  25.3 7.7 all-to-all-start
  36.5 4.0 fusion.34
  42.5 5.7 fusion.78
  48.2 6.4 copy.222
  55.3 4.4 fusion.84
  59.7 2.1 fusion.3
  62.1 6.4 copy.225
  69.0 4.4 fusion.10
  73.4 12.4 %all-to-all-done = bf16[32,2,64,512]{3,2,1,0:T(8,128)(2,1)} async-done(((bf16[32,2,64,512]{3,2,1,0:T(8,128)(2,1)}), bf16[32,2,64,512]{3,2,1,0:T(8,128)(2,1)}, u32[]{:S(2)}, u32[]{:S(2)}) %all-to-all-start) | async-done | bytes 4194336 | tf_op jit(solution)/shard_map/all_to_all | solution.py:140
  85.7 4.2 gather_fusion.4
  90.0 2.7 fusion.79
  92.7 2.2 reshape_squeeze.15
  102.8 2.0 collective-permute-start
  104.8 6.1 collective-permute-done
  110.9 3.8 collective-permute-start.1
  114.7 5.2 collective-permute-done.1
  121.3 46.8 %all-gather.2.cloned.1.call-done = bf16[1024,2048]{1,0:T(8,128)(2,1)} async-done(((bf16[32,2048]{1,0:T(8,128)(2,1)}), bf16[1024,2048]{1,0:T(8,128)(2,1)}) %all-gather.2.cloned.1.call-update) | async-done | bytes 4194320 | tf_op jit(solution)/shard_map/all_gather | solution.py:160
  168.1 3.6 fusion.85
  171.7 8.0 fusion.6
  179.7 651.6 %reduce-scatter.2.cloned.1.call-done = f32[8,2048]{1,0:T(8,128)} async-done(((f32[1024,2048]{1,0:T(8,128)}), f32[8,2048]{1,0:T(8,128)}) %reduce-scatter.2.cloned.1.call-update) | async-done | bytes 65552 | tf_op jit(solution)/shard_map/reduce_scatter | solution.py:161
  833.3 2.1 multiply_reduce_fusion
  (104 shorter events, 23.7 us)
Async XLA Ops:
  7.2 95.1 %copy-start = (bf16[512,2048]{1,0:T(8,128)(2,1)S(1)}, bf16[512,2048]{1,0:T(8,128)(2,1)}, u32[]{:S(2)}) copy-start(bf16[512,2048]{1,0:T(8,128)(2,1)} %param.19) | copy-start | bytes 6291460
  25.3 8.5 %copy-start.1 = (s32[512]{0:T(512)S(1)}, s32[512]{0:T(512)}, u32[]{:S(2)}) copy-start(s32[512]{0:T(512)} %param.15) | copy-start | bytes 6148
  25.3 9.2 %copy-start.9 = (s32[32]{0:T(128)S(1)}, s32[32]{0:T(128)}, u32[]{:S(2)}) copy-start(s32[32]{0:T(128)} %param.13) | copy-start | bytes 388
  25.3 9.8 %copy-start.8 = (s32[32,16]{0,1:T(8,128)S(1)}, s32[32,16]{0,1:T(8,128)}, u32[]{:S(2)}) copy-start(s32[32,16]{0,1:T(8,128)} %param.14) | copy-start | bytes 6148
  25.3 10.0 %copy-start.2 = (bf16[32,2048]{1,0:T(8,128)(2,1)S(1)}, bf16[32,2048]{1,0:T(8,128)(2,1)}, u32[]{:S(2)}) copy-start(bf16[32,2048]{1,0:T(8,128)(2,1)} %param.12) | copy-start | bytes 393220
  25.3 60.4 %all-to-all-start = ((bf16[32,2,64,512]{3,2,1,0:T(8,128)(2,1)}), bf16[32,2,64,512]{3,2,1,0:T(8,128)(2,1)}, u32[]{:S(2)}, u32[]{:S(2)}) async-start(bf16[32,2,64,512]{3,2,1,0:T(8,128)(2,1)} %scatter_fusion), calls=%async_computation | async-start | bytes 8388608 | tf_op jit(solution)/shard_map/all_to_all | solution.py:140
  33.0 135.1 %all-gather.2.cloned.1.call-start = ((), (), s32[]{:S(2)}) async-start(), calls=%async_computation.2 | async-start | bytes 4325376 | tf_op jit(solution)/shard_map/all_gather | solution.py:160
  68.8 26.1 %copy-start.6 = (pred[16,64]{1,0:T(8,128)(4,1)}, pred[16,64]{1,0:T(8,128)(4,1)S(1)}, u32[]{:S(2)}) copy-start(pred[16,64]{1,0:T(8,128)(4,1)S(1)} %iota_compare_fusion.3) | copy-start | bytes 3076
  99.7 68.4 %copy-start.3 = (bf16[64,2048]{1,0:T(8,128)(2,1)S(1)}, bf16[64,2048]{1,0:T(8,128)(2,1)}, u32[]{:S(2)}) copy-start(bf16[64,2048]{1,0:T(8,128)(2,1)} %param.20) | copy-start | bytes 786436
  102.8 68.9 %copy-start.4 = (bf16[64,2048]{1,0:T(8,128)(2,1)S(1)}, bf16[64,2048]{1,0:T(8,128)(2,1)}, u32[]{:S(2)}) copy-start(bf16[64,2048]{1,0:T(8,128)(2,1)} %param.22) | copy-start | bytes 786436
  102.8 68.9 %copy-start.5 = (bf16[64,2048]{1,0:T(8,128)(2,1)S(1)}, bf16[64,2048]{1,0:T(8,128)(2,1)}, u32[]{:S(2)}) copy-start(bf16[64,2048]{1,0:T(8,128)(2,1)} %param.21) | copy-start | bytes 786436
  102.8 8.1 collective-permute-start
  110.9 9.0 %collective-permute-start.1 = (f32[32,2048]{1,0:T(8,128)S(1)}, f32[32,2048]{1,0:T(8,128)S(1)}, u32[]{:S(2)}, u32[]{:S(2)}) collective-permute-start(f32[32,2048]{1,0:T(8,128)S(1)} %add.250), channel_id=1, source_target_pairs={{0,2},{1,3},{2,0},{3,1},{4,6},{5,7},{6,4},{7,5},{8,10},{9,11},{10,... | collective-permute-start | bytes 786440 | tf_op jit(solution)/shard_map/ppermute | solution.py:155
  121.1 710.2 %reduce-scatter.2.cloned.1.call-start = ((), (), s32[]{:S(2)}) async-start(), calls=%async_computation.3 | async-start | bytes 8454144 | tf_op jit(solution)/shard_map/reduce_scatter | solution.py:161
  179.6 653.6 %copy-start.7 = (f32[2048]{0:T(1024)S(1)}, f32[2048]{0:T(1024)}, u32[]{:S(2)}) copy-start(f32[2048]{0:T(1024)} %param.23) | copy-start | bytes 24580
Sparse Core Ops, SparseCore 0:
  121.2 46.8 all-gather.1
  179.8 651.4 reduce-scatter.1
